TPU v7x, 32 devices: a whole 2x2x4 slice. The times are simulated.
32 devices in a mesh: doc: 4 (over y, x), cen: 8 (over z, core).
Axes of the slice: x: 2, y: 2, z: 4, core: 2. Of those that a mesh axis runs over, the one named last changes fastest.
Arguments:
- passages: bfloat16 [1536, 1024], P(('doc', 'cen')), may hold values from -64 to 64
- centroids: bfloat16 [8192, 1024], P('cen'), may hold values from -64 to 64
Outputs:
- assign: bfloat16 [1536, 8192], P('doc', 'cen')
- masses: float32 [8192], P('cen')
- new_centroids: float32 [8192, 1024], P('cen', 'doc')
All inputs are finite; a program needn't handle non-finite values.
Results may differ from a plain program's by a relative error of at most 0.008.
Values may be sent and summed in bfloat16 or wider, within the bound.
A program may use at most 64 MiB of HBM per device.

v0:
```python
import math
import jax
import jax.numpy as jnp
from jax import lax
from jax.sharding import PartitionSpec as P

ITERS = 3


def row_log_total(shifted):
    local_max = jnp.max(shifted, axis=1)
    peak = lax.pmax(local_max, "cen")
    total = lax.psum(jnp.sum(jnp.exp(shifted - peak[:, None]), axis=1), "cen")
    return peak + jnp.log(total)


def col_log_total(shifted):
    local_max = jnp.max(shifted, axis=0)
    peak = lax.pmax(local_max, "doc")
    total = lax.psum(jnp.sum(jnp.exp(shifted - peak[None, :]), axis=0), "doc")
    return peak + jnp.log(total)


def shards(passages, centroids):
    cen_count = lax.axis_size("cen")
    doc_count = lax.axis_size("doc")
    width = passages.shape[1]
    scale = 1.0 / math.sqrt(width)
    group_rows = lax.all_gather(passages, "cen", axis=0, tiled=True)
    scores = (
        lax.dot_general(
            group_rows, centroids, (((1,), (1,)), ((), ())), preferred_element_type=jnp.float32
        )
        * scale
    )
    local_cols = centroids.shape[0]
    total_cols = local_cols * cen_count
    total_rows = scores.shape[0] * doc_count
    log_column = math.log(total_rows / total_cols)
    col_potential = jnp.zeros((local_cols,), jnp.float32)
    for iteration in range(ITERS):
        row_potential = -row_log_total(scores + col_potential[None, :])
        col_potential = log_column - col_log_total(scores + row_potential[:, None])
    row_potential = -row_log_total(scores + col_potential[None, :])
    weights = jnp.exp(scores + row_potential[:, None] + col_potential[None, :])
    assign = (weights * total_cols).astype(jnp.bfloat16)
    raw_mass = lax.psum(jnp.sum(weights, axis=0), "doc")
    partial_value = lax.dot_general(
        assign, group_rows, (((0,), (0,)), ((), ())), preferred_element_type=jnp.float32
    )
    sums = lax.psum_scatter(
        partial_value.astype(jnp.bfloat16), "doc", scatter_dimension=1, tiled=True
    ).astype(jnp.float32)
    new_centroids = sums / total_cols / raw_mass[:, None]
    masses = raw_mass * total_cols / total_rows
    return (assign, masses, new_centroids)


def solution(mesh):
    in_specs = (P(("doc", "cen"), None), P("cen", None))
    out_specs = (P("doc", "cen"), P("cen"), P("cen", "doc"))
    return jax.shard_map(shards, mesh=mesh, in_specs=in_specs, out_specs=out_specs, check_vma=False)
```

profile of v0, /device:TPU:0, one launch (start us, length us, event | category | flops | bytes accessed | tf_op | source)
XLA Modules:
  0.0 261.0 jit_solution(13473562070455772774)
XLA Ops:
  7.2 0.0 copy-start
  7.2 0.0 reduce-scatter.2.cloned.1.call-start
  7.2 17.6 %all_gather.3 = bf16[384,1024]{1,0:T(8,128)(2,1)S(1)} all-gather(bf16[48,1024]{1,0:T(8,128)(2,1)} %param.2), channel_id=1, replica_groups=mesh['doc'=4,'cen'=8] {'cen'}, dimensions={0}, use_global_device_ids=true | all-gather | bytes 884736 | tf_op jit(solution)/shard_map/all_gather | solution.py:29
  24.8 0.0 copy-done
  24.8 2.2 fusion.1
  27.0 17.0 %pmax.49 = f32[384]{0:T(512)S(1)} all-reduce(f32[384]{0:T(512)S(1)} %get-tuple-element.5), channel_id=1, replica_groups=mesh['doc'=4,'cen'=8] {'cen'}, use_global_device_ids=true, to_apply=%region_1.0 | all-reduce | flops 384 | bytes 3072 | tf_op jit(solution)/shard_map/pmax | solution.py:12
  44.0 1.8 exponential_reduce_fusion.6
  45.8 13.6 %psum.56 = f32[384]{0:T(512)S(1)} all-reduce(f32[384]{0:T(512)S(1)} %exponential_reduce_fusion.6), channel_id=1, replica_groups=mesh['doc'=4,'cen'=8] {'cen'}, use_global_device_ids=true, to_apply=%region_3.0 | all-reduce | flops 384 | bytes 3072 | tf_op jit(solution)/shard_map/psum | solution.py:13
  59.4 1.6 add_reduce_fusion.5
  61.0 9.9 %pmax.50 = f32[1024]{0:T(1024)S(1)} all-reduce(f32[1024]{0:T(1024)S(1)} %add_reduce_fusion.5), channel_id=1, replica_groups=mesh['doc'=4,'cen'=8] {'doc'}, use_global_device_ids=true, to_apply=%region_5.0 | all-reduce | flops 1024 | bytes 8192 | tf_op jit(solution)/shard_map/pmax | solution.py:19
  70.9 1.7 exponential_reduce_fusion.5
  72.7 8.0 %psum.57 = f32[1024]{0:T(1024)S(1)} all-reduce(f32[1024]{0:T(1024)S(1)} %exponential_reduce_fusion.5), channel_id=1, replica_groups=mesh['doc'=4,'cen'=8] {'doc'}, use_global_device_ids=true, to_apply=%region_7.0 | all-reduce | flops 1024 | bytes 8192 | tf_op jit(solution)/shard_map/psum | solution.py:20
  80.7 1.6 add_reduce_fusion.4
  82.3 13.6 %pmax.51 = f32[384]{0:T(512)S(1)} all-reduce(f32[384]{0:T(512)S(1)} %add_reduce_fusion.4), channel_id=1, replica_groups=mesh['doc'=4,'cen'=8] {'cen'}, use_global_device_ids=true, to_apply=%region_9.0 | all-reduce | flops 384 | bytes 3072 | tf_op jit(solution)/shard_map/pmax | solution.py:12
  95.8 1.8 exponential_reduce_fusion.4
  97.7 13.6 %psum.58 = f32[384]{0:T(512)S(1)} all-reduce(f32[384]{0:T(512)S(1)} %exponential_reduce_fusion.4), channel_id=1, replica_groups=mesh['doc'=4,'cen'=8] {'cen'}, use_global_device_ids=true, to_apply=%region_11.0 | all-reduce | flops 384 | bytes 3072 | tf_op jit(solution)/shard_map/psum | solution.py:13
  111.3 1.6 add_reduce_fusion.3
  112.8 9.0 %pmax.52 = f32[1024]{0:T(1024)S(1)} all-reduce(f32[1024]{0:T(1024)S(1)} %add_reduce_fusion.3), channel_id=1, replica_groups=mesh['doc'=4,'cen'=8] {'doc'}, use_global_device_ids=true, to_apply=%region_13.0 | all-reduce | flops 1024 | bytes 8192 | tf_op jit(solution)/shard_map/pmax | solution.py:19
  121.8 1.7 exponential_reduce_fusion.3
  123.6 8.0 %psum.59 = f32[1024]{0:T(1024)S(1)} all-reduce(f32[1024]{0:T(1024)S(1)} %exponential_reduce_fusion.3), channel_id=1, replica_groups=mesh['doc'=4,'cen'=8] {'doc'}, use_global_device_ids=true, to_apply=%region_15.0 | all-reduce | flops 1024 | bytes 8192 | tf_op jit(solution)/shard_map/psum | solution.py:20
  131.6 1.6 add_reduce_fusion.2
  133.2 13.6 %pmax.53 = f32[384]{0:T(512)S(1)} all-reduce(f32[384]{0:T(512)S(1)} %add_reduce_fusion.2), channel_id=1, replica_groups=mesh['doc'=4,'cen'=8] {'cen'}, use_global_device_ids=true, to_apply=%region_17.0 | all-reduce | flops 384 | bytes 3072 | tf_op jit(solution)/shard_map/pmax | solution.py:12
  146.8 1.8 exponential_reduce_fusion.2
  148.6 13.6 %psum.60 = f32[384]{0:T(512)S(1)} all-reduce(f32[384]{0:T(512)S(1)} %exponential_reduce_fusion.2), channel_id=1, replica_groups=mesh['doc'=4,'cen'=8] {'cen'}, use_global_device_ids=true, to_apply=%region_19.0 | all-reduce | flops 384 | bytes 3072 | tf_op jit(solution)/shard_map/psum | solution.py:13
  162.2 1.6 add_reduce_fusion.1
  163.8 9.7 %pmax.54 = f32[1024]{0:T(1024)S(1)} all-reduce(f32[1024]{0:T(1024)S(1)} %add_reduce_fusion.1), channel_id=1, replica_groups=mesh['doc'=4,'cen'=8] {'doc'}, use_global_device_ids=true, to_apply=%region_21.0 | all-reduce | flops 1024 | bytes 8192 | tf_op jit(solution)/shard_map/pmax | solution.py:19
  173.5 1.7 exponential_reduce_fusion.1
  175.3 8.0 %psum.61 = f32[1024]{0:T(1024)S(1)} all-reduce(f32[1024]{0:T(1024)S(1)} %exponential_reduce_fusion.1), channel_id=1, replica_groups=mesh['doc'=4,'cen'=8] {'doc'}, use_global_device_ids=true, to_apply=%region_23.0 | all-reduce | flops 1024 | bytes 8192 | tf_op jit(solution)/shard_map/psum | solution.py:20
  183.4 1.6 add_reduce_fusion
  184.9 13.6 %pmax.55 = f32[384]{0:T(512)S(1)} all-reduce(f32[384]{0:T(512)S(1)} %add_reduce_fusion), channel_id=1, replica_groups=mesh['doc'=4,'cen'=8] {'cen'}, use_global_device_ids=true, to_apply=%region_25.0 | all-reduce | flops 384 | bytes 3072 | tf_op jit(solution)/shard_map/pmax | solution.py:12
  198.5 1.8 exponential_reduce_fusion
  200.3 13.6 %psum.62 = f32[384]{0:T(512)S(1)} all-reduce(f32[384]{0:T(512)S(1)} %exponential_reduce_fusion), channel_id=1, replica_groups=mesh['doc'=4,'cen'=8] {'cen'}, use_global_device_ids=true, to_apply=%region_27.0 | all-reduce | flops 384 | bytes 3072 | tf_op jit(solution)/shard_map/psum | solution.py:13
  213.9 1.8 fusion
  215.8 0.0 copy-start.1
  215.8 0.9 copy-done.1
  216.7 2.6 %convolution_convert_fusion = bf16[1024,1024]{1,0:T(8,128)(2,1)} fusion(bf16[384,1024]{1,0:T(8,128)(2,1)S(1)} %get-tuple-element.4, bf16[384,1024]{1,0:T(8,128)(2,1)S(1)} %all_gather.3), kind=kOutput, calls=%fused_computation | convolution fusion | flops 806354944 | bytes 3670016 | tf_op jit(solution)/shard_map/dot_general | solution.py:48
  219.3 0.0 reduce-scatter.2.cloned.1.call-update
  219.3 9.0 %psum.63 = f32[1024]{0:T(1024)S(1)} all-reduce(f32[1024]{0:T(1024)S(1)} %get-tuple-element.3), channel_id=1, replica_groups=mesh['doc'=4,'cen'=8] {'doc'}, use_global_device_ids=true, to_apply=%region_29.0 | all-reduce | flops 1024 | bytes 8192 | tf_op jit(solution)/shard_map/psum | solution.py:47
  228.4 0.6 broadcast_multiply_fusion
  229.0 22.9 %reduce-scatter.2.cloned.1.call-done = bf16[1024,256]{1,0:T(8,128)(2,1)} async-done(((bf16[1024,1024]{1,0:T(8,128)(2,1)}), bf16[1024,256]{1,0:T(8,128)(2,1)}) %reduce-scatter.2.cloned.1.call-update) | async-done | bytes 524304 | tf_op jit(solution)/shard_map/reduce_scatter | solution.py:51
  251.9 2.2 multiply_divide_fusion
  (7 shorter events, 0.1 us)
Async XLA Ops:
  7.2 17.6 %copy-start = (bf16[1024,1024]{1,0:T(8,128)(2,1)S(1)}, bf16[1024,1024]{1,0:T(8,128)(2,1)}, u32[]{:S(2)}) copy-start(bf16[1024,1024]{1,0:T(8,128)(2,1)} %param.3) | copy-start | bytes 6291460
  7.2 244.7 %reduce-scatter.2.cloned.1.call-start = ((), (), s32[]{:S(2)}) async-start(), calls=%async_computation.1 | async-start | bytes 2621440 | tf_op jit(solution)/shard_map/reduce_scatter | solution.py:51
  215.8 0.9 copy-start.1
Sparse Core Ops, SparseCore 0:
  219.4 32.4 reduce-scatter.1
where the time goes:
time: 262 us; the launch traced here: 261 us
  blocking collectives  191 us (73%)
  other arithmetic  26.7 us (10%)
  waiting for transfers between devices  23 us (9%)
  between operations  14.1 us (5%)
  matrix products  4.81 us (2%)
    pmax x4, blocking collectives, row_log_total(): peak = lax.pmax(local_max, 'cen')  57.8 us
    psum x4, blocking collectives, row_log_total(): total = lax.psum(jnp.sum(jnp.exp(shifted - peak[:, None]), axis=1), 'cen')  54.4 us
    pmax x3, blocking collectives, col_log_total(): peak = lax.pmax(local_max, 'doc')  28.6 us
    psum x3, blocking collectives, col_log_total(): total = lax.psum(jnp.sum(jnp.exp(shifted - peak[None, :]), axis=0), 'doc')  24.1 us
    reduce_scatter x1, waiting for transfers between devices, shards(): lax.psum_scatter(partial_value.astype(jnp.bfloat16), 'doc', scatter_dimen...  22.9 us
    all_gather x1, blocking collectives, shards(): group_rows = lax.all_gather(passages, 'cen', axis=0, tiled=True)  17.6 us
    psum x1, blocking collectives, shards(): raw_mass = lax.psum(jnp.sum(weights, axis=0), 'doc')  9.04 us
    reduce_sum x4, other arithmetic, row_log_total(): total = lax.psum(jnp.sum(jnp.exp(shifted - peak[:, None]), axis=1), 'cen')  7.19 us
  transfers between devices with their start and end apart: 1, of which 1 were waited for; matrix products, arithmetic and copies ran while one was open for 0% of the time, Pallas kernels for 0%

commit v1 on v0

--- a/solution.py
+++ b/solution.py
@@ -26,7 +26,16 @@
     doc_count = lax.axis_size("doc")
     width = passages.shape[1]
     scale = 1.0 / math.sqrt(width)
-    group_rows = lax.all_gather(passages, "cen", axis=0, tiled=True)
+    passed, outcome_arr = (jax.lax.axis_size("cen"), jax.lax.axis_index("cen"))
+    group_rows, r1 = (passages, 1)
+    while r1 < passed:
+        y_new = jax.lax.ppermute(
+            group_rows, axis_name="cen", perm=[(j, j ^ r1) for j in range(passed)]
+        )
+        item_now = jnp.concatenate([group_rows, y_new], axis=0)
+        arr_now = jnp.concatenate([y_new, group_rows], axis=0)
+        group_rows = jnp.where(outcome_arr & r1 == 0, item_now, arr_now)
+        r1 = 2 * r1
     scores = (
         lax.dot_general(
             group_rows, centroids, (((1,), (1,)), ((), ())), preferred_element_type=jnp.float32

time: 262 us -> 274 us (1.046)
  waiting for transfers between devices: 23 us -> 46.6 us
  blocking collectives: 191 us -> 173 us
  starting transfers between devices: 0.04 us -> 6.37 us
    ppermute x0 -> x3, waiting for transfers between devices: none -> 23.6 us  [shards(): jax.lax.ppermute(group_rows, axis_name='cen', perm=[(j, j ^ r1) for j in...]
    all_gather x1 -> x0, blocking collectives: 17.6 us -> none  [shards(): group_rows = lax.all_gather(passages, 'cen', axis=0, tiled=True)]
    ppermute x0 -> x3, starting transfers between devices: none -> 6.33 us  [shards(): jax.lax.ppermute(group_rows, axis_name='cen', perm=[(j, j ^ r1) for j in...]
  transfers between devices with their start and end apart: 1 -> 4, of which waited for: 1 -> 4; matrix products, arithmetic and copies ran while one was open for 0% -> 0% of each run, Pallas kernels for 0% -> 0%
where the time goes in v1:
time: 274 us; the launch traced here: 273 us
  blocking collectives  173 us (63%)
  waiting for transfers between devices  46.6 us (17%)
  other arithmetic  27.8 us (10%)
  between operations  14.1 us (5%)
  starting transfers between devices  6.37 us (2%)
  matrix products  4.87 us (2%)
    pmax x4, blocking collectives, row_log_total(): peak = lax.pmax(local_max, 'cen')  57.3 us
    psum x4, blocking collectives, row_log_total(): total = lax.psum(jnp.sum(jnp.exp(shifted - peak[:, None]), axis=1), 'cen')  54.4 us
    pmax x3, blocking collectives, col_log_total(): peak = lax.pmax(local_max, 'doc')  28.6 us
    psum x3, blocking collectives, col_log_total(): total = lax.psum(jnp.sum(jnp.exp(shifted - peak[None, :]), axis=0), 'doc')  24.1 us
    ppermute x3, waiting for transfers between devices, shards(): jax.lax.ppermute(group_rows, axis_name='cen', perm=[(j, j ^ r1) for j in...  23.6 us
    reduce_scatter x1, waiting for transfers between devices, shards(): lax.psum_scatter(partial_value.astype(jnp.bfloat16), 'doc', scatter_dimen...  22.9 us
    psum x1, blocking collectives, shards(): raw_mass = lax.psum(jnp.sum(weights, axis=0), 'doc')  9.04 us
    reduce_sum x4, other arithmetic, row_log_total(): total = lax.psum(jnp.sum(jnp.exp(shifted - peak[:, None]), axis=1), 'cen')  7.19 us
  transfers between devices with their start and end apart: 4, of which 4 were waited for; matrix products, arithmetic and copies ran while one was open for 0% of the time, Pallas kernels for 0%

profile of v1, /device:TPU:0, one launch (start us, length us, event | category | flops | bytes accessed | tf_op | source)
XLA Modules:
  0.0 273.2 jit_solution(15502789089456203110)
XLA Ops:
  7.2 0.0 copy-start
  7.2 0.0 reduce-scatter.2.cloned.1.call-start
  7.2 0.5 collective-permute-start
  7.7 1.2 collective-permute-done
  8.9 1.0 maximum_select_fusion.2
  9.9 3.0 %collective-permute-start.1 = (bf16[96,1024]{1,0:T(8,128)(2,1)S(1)}, bf16[96,1024]{1,0:T(8,128)(2,1)S(1)}, u32[]{:S(2)}, u32[]{:S(2)}) collective-permute-start(bf16[96,1024]{1,0:T(8,128)(2,1)S(1)} %maximum_select_fusion.2), channel_id=1, source_target_pairs={{0,2},{1,3},{2,0},{3,1},{4,6},{5,7},{6,4},{7,5},{8,10},{9,11},{10,... | collective-permute-start | bytes 589832 | tf_op jit(solution)/shard_map/ppermute | solution.py:32
  12.9 5.2 %collective-permute-done.1 = bf16[96,1024]{1,0:T(8,128)(2,1)S(1)} collective-permute-done((bf16[96,1024]{1,0:T(8,128)(2,1)S(1)}, bf16[96,1024]{1,0:T(8,128)(2,1)S(1)}, u32[]{:S(2)}, u32[]{:S(2)}) %collective-permute-start.1) | collective-permute-done | bytes 196640 | tf_op jit(solution)/shard_map/ppermute | solution.py:32
  18.1 0.1 maximum_select_fusion.1
  18.2 2.8 %collective-permute-start.2 = (bf16[192,1024]{1,0:T(8,128)(2,1)S(1)}, bf16[192,1024]{1,0:T(8,128)(2,1)S(1)}, u32[]{:S(2)}, u32[]{:S(2)}) collective-permute-start(bf16[192,1024]{1,0:T(8,128)(2,1)S(1)} %maximum_select_fusion.1), channel_id=1, source_target_pairs={{0,4},{1,5},{2,6},{3,7},{4,0},{5,1},{6,2},{7,3},{8,12},{9,13},{10,... | collective-permute-start | bytes 1179656 | tf_op jit(solution)/shard_map/ppermute | solution.py:32
  21.0 17.2 %collective-permute-done.2 = bf16[192,1024]{1,0:T(8,128)(2,1)S(1)} collective-permute-done((bf16[192,1024]{1,0:T(8,128)(2,1)S(1)}, bf16[192,1024]{1,0:T(8,128)(2,1)S(1)}, u32[]{:S(2)}, u32[]{:S(2)}) %collective-permute-start.2) | collective-permute-done | bytes 393248 | tf_op jit(solution)/shard_map/ppermute | solution.py:32
  38.3 0.0 copy-done
  38.3 2.2 fusion.3
  40.5 16.5 %pmax.49 = f32[384]{0:T(512)S(1)} all-reduce(f32[384]{0:T(512)S(1)} %get-tuple-element.5), channel_id=1, replica_groups=mesh['doc'=4,'cen'=8] {'cen'}, use_global_device_ids=true, to_apply=%region_1.2 | all-reduce | flops 384 | bytes 3072 | tf_op jit(solution)/shard_map/pmax | solution.py:12
  57.0 1.8 exponential_reduce_fusion.6
  58.8 13.6 %psum.56 = f32[384]{0:T(512)S(1)} all-reduce(f32[384]{0:T(512)S(1)} %exponential_reduce_fusion.6), channel_id=1, replica_groups=mesh['doc'=4,'cen'=8] {'cen'}, use_global_device_ids=true, to_apply=%region_3.4 | all-reduce | flops 384 | bytes 3072 | tf_op jit(solution)/shard_map/psum | solution.py:13
  72.4 1.6 add_reduce_fusion.5
  74.0 9.9 %pmax.50 = f32[1024]{0:T(1024)S(1)} all-reduce(f32[1024]{0:T(1024)S(1)} %add_reduce_fusion.5), channel_id=1, replica_groups=mesh['doc'=4,'cen'=8] {'doc'}, use_global_device_ids=true, to_apply=%region_5.6 | all-reduce | flops 1024 | bytes 8192 | tf_op jit(solution)/shard_map/pmax | solution.py:19
  83.9 1.7 exponential_reduce_fusion.5
  85.6 8.0 %psum.57 = f32[1024]{0:T(1024)S(1)} all-reduce(f32[1024]{0:T(1024)S(1)} %exponential_reduce_fusion.5), channel_id=1, replica_groups=mesh['doc'=4,'cen'=8] {'doc'}, use_global_device_ids=true, to_apply=%region_7.8 | all-reduce | flops 1024 | bytes 8192 | tf_op jit(solution)/shard_map/psum | solution.py:20
  93.7 1.6 add_reduce_fusion.4
  95.3 13.6 %pmax.51 = f32[384]{0:T(512)S(1)} all-reduce(f32[384]{0:T(512)S(1)} %add_reduce_fusion.4), channel_id=1, replica_groups=mesh['doc'=4,'cen'=8] {'cen'}, use_global_device_ids=true, to_apply=%region_9.10 | all-reduce | flops 384 | bytes 3072 | tf_op jit(solution)/shard_map/pmax | solution.py:12
  108.8 1.8 exponential_reduce_fusion.4
  110.6 13.6 %psum.58 = f32[384]{0:T(512)S(1)} all-reduce(f32[384]{0:T(512)S(1)} %exponential_reduce_fusion.4), channel_id=1, replica_groups=mesh['doc'=4,'cen'=8] {'cen'}, use_global_device_ids=true, to_apply=%region_11.12 | all-reduce | flops 384 | bytes 3072 | tf_op jit(solution)/shard_map/psum | solution.py:13
  124.2 1.6 add_reduce_fusion.3
  125.8 9.0 %pmax.52 = f32[1024]{0:T(1024)S(1)} all-reduce(f32[1024]{0:T(1024)S(1)} %add_reduce_fusion.3), channel_id=1, replica_groups=mesh['doc'=4,'cen'=8] {'doc'}, use_global_device_ids=true, to_apply=%region_13.14 | all-reduce | flops 1024 | bytes 8192 | tf_op jit(solution)/shard_map/pmax | solution.py:19
  134.8 1.7 exponential_reduce_fusion.3
  136.5 8.1 %psum.59 = f32[1024]{0:T(1024)S(1)} all-reduce(f32[1024]{0:T(1024)S(1)} %exponential_reduce_fusion.3), channel_id=1, replica_groups=mesh['doc'=4,'cen'=8] {'doc'}, use_global_device_ids=true, to_apply=%region_15.16 | all-reduce | flops 1024 | bytes 8192 | tf_op jit(solution)/shard_map/psum | solution.py:20
  144.6 1.6 add_reduce_fusion.2
  146.2 13.6 %pmax.53 = f32[384]{0:T(512)S(1)} all-reduce(f32[384]{0:T(512)S(1)} %add_reduce_fusion.2), channel_id=1, replica_groups=mesh['doc'=4,'cen'=8] {'cen'}, use_global_device_ids=true, to_apply=%region_17.18 | all-reduce | flops 384 | bytes 3072 | tf_op jit(solution)/shard_map/pmax | solution.py:12
  159.8 1.8 exponential_reduce_fusion.2
  161.6 13.6 %psum.60 = f32[384]{0:T(512)S(1)} all-reduce(f32[384]{0:T(512)S(1)} %exponential_reduce_fusion.2), channel_id=1, replica_groups=mesh['doc'=4,'cen'=8] {'cen'}, use_global_device_ids=true, to_apply=%region_19.20 | all-reduce | flops 384 | bytes 3072 | tf_op jit(solution)/shard_map/psum | solution.py:13
  175.2 1.6 add_reduce_fusion.1
  176.8 9.7 %pmax.54 = f32[1024]{0:T(1024)S(1)} all-reduce(f32[1024]{0:T(1024)S(1)} %add_reduce_fusion.1), channel_id=1, replica_groups=mesh['doc'=4,'cen'=8] {'doc'}, use_global_device_ids=true, to_apply=%region_21.22 | all-reduce | flops 1024 | bytes 8192 | tf_op jit(solution)/shard_map/pmax | solution.py:19
  186.5 1.7 exponential_reduce_fusion.1
  188.3 8.1 %psum.61 = f32[1024]{0:T(1024)S(1)} all-reduce(f32[1024]{0:T(1024)S(1)} %exponential_reduce_fusion.1), channel_id=1, replica_groups=mesh['doc'=4,'cen'=8] {'doc'}, use_global_device_ids=true, to_apply=%region_23.24 | all-reduce | flops 1024 | bytes 8192 | tf_op jit(solution)/shard_map/psum | solution.py:20
  196.3 1.6 add_reduce_fusion
  197.9 13.6 %pmax.55 = f32[384]{0:T(512)S(1)} all-reduce(f32[384]{0:T(512)S(1)} %add_reduce_fusion), channel_id=1, replica_groups=mesh['doc'=4,'cen'=8] {'cen'}, use_global_device_ids=true, to_apply=%region_25.26 | all-reduce | flops 384 | bytes 3072 | tf_op jit(solution)/shard_map/pmax | solution.py:12
  211.5 1.8 exponential_reduce_fusion
  213.3 13.6 %psum.62 = f32[384]{0:T(512)S(1)} all-reduce(f32[384]{0:T(512)S(1)} %exponential_reduce_fusion), channel_id=1, replica_groups=mesh['doc'=4,'cen'=8] {'cen'}, use_global_device_ids=true, to_apply=%region_27.28 | all-reduce | flops 384 | bytes 3072 | tf_op jit(solution)/shard_map/psum | solution.py:13
  226.9 1.9 fusion
  228.8 0.0 copy-start.1
  228.8 2.7 convolution_convert_fusion
  231.5 0.0 copy-done.1
  231.5 0.0 reduce-scatter.2.cloned.1.call-update
  231.5 9.0 %psum.63 = f32[1024]{0:T(1024)S(1)} all-reduce(f32[1024]{0:T(1024)S(1)} %get-tuple-element.3), channel_id=1, replica_groups=mesh['doc'=4,'cen'=8] {'doc'}, use_global_device_ids=true, to_apply=%region_29.30 | all-reduce | flops 1024 | bytes 8192 | tf_op jit(solution)/shard_map/psum | solution.py:56
  240.6 0.6 broadcast_multiply_fusion
  241.2 22.9 %reduce-scatter.2.cloned.1.call-done = bf16[1024,256]{1,0:T(8,128)(2,1)} async-done(((bf16[1024,1024]{1,0:T(8,128)(2,1)}), bf16[1024,256]{1,0:T(8,128)(2,1)}) %reduce-scatter.2.cloned.1.call-update) | async-done | bytes 524304 | tf_op jit(solution)/shard_map/reduce_scatter | solution.py:60
  264.1 2.2 multiply_divide_fusion
  (11 shorter events, 0.1 us)
Async XLA Ops:
  7.2 31.1 %copy-start = (bf16[1024,1024]{1,0:T(8,128)(2,1)S(1)}, bf16[1024,1024]{1,0:T(8,128)(2,1)}, u32[]{:S(2)}) copy-start(bf16[1024,1024]{1,0:T(8,128)(2,1)} %param.3) | copy-start | bytes 6291460
  7.2 256.9 %reduce-scatter.2.cloned.1.call-start = ((), (), s32[]{:S(2)}) async-start(), calls=%async_computation.1 | async-start | bytes 2621440 | tf_op jit(solution)/shard_map/reduce_scatter | solution.py:60
  7.2 1.7 collective-permute-start
  9.9 8.2 %collective-permute-start.1 = (bf16[96,1024]{1,0:T(8,128)(2,1)S(1)}, bf16[96,1024]{1,0:T(8,128)(2,1)S(1)}, u32[]{:S(2)}, u32[]{:S(2)}) collective-permute-start(bf16[96,1024]{1,0:T(8,128)(2,1)S(1)} %maximum_select_fusion.2), channel_id=1, source_target_pairs={{0,2},{1,3},{2,0},{3,1},{4,6},{5,7},{6,4},{7,5},{8,10},{9,11},{10,... | collective-permute-start | bytes 589832 | tf_op jit(solution)/shard_map/ppermute | solution.py:32
  18.2 20.1 %collective-permute-start.2 = (bf16[192,1024]{1,0:T(8,128)(2,1)S(1)}, bf16[192,1024]{1,0:T(8,128)(2,1)S(1)}, u32[]{:S(2)}, u32[]{:S(2)}) collective-permute-start(bf16[192,1024]{1,0:T(8,128)(2,1)S(1)} %maximum_select_fusion.1), channel_id=1, source_target_pairs={{0,4},{1,5},{2,6},{3,7},{4,0},{5,1},{6,2},{7,3},{8,12},{9,13},{10,... | collective-permute-start | bytes 1179656 | tf_op jit(solution)/shard_map/ppermute | solution.py:32
  38.3 2.2 copy-start.2
  226.9 1.9 copy-start.3
  228.8 2.7 copy-start.1
Sparse Core Ops, SparseCore 0:
  231.6 32.4 reduce-scatter.1
